TPU v7x, 512 devices: a whole 4x8x8 slice. The times are simulated.
512 devices in a mesh: pair: 32 (over y, x), row: 16 (over z, core).
Axes of the slice: x: 4, y: 8, z: 8, core: 2. Of those that a mesh axis runs over, the one named last changes fastest.
Arguments:
- r_factor: float32 [16384, 16384], P(('row', 'pair')), may hold values from -40 to 40, as said below
- block_slots: int32 [256], replicated, may hold values from 0 to 255, as said below
Outputs:
- rotated: float32 [16384, 16384], P('row', 'pair')
- off_ratio: float32 [], replicated
Inputs may be any that keep to these rules, and one draw needn't show every extreme that they name: `block_slots`: each of the 256 column blocks appears exactly once. `r_factor`: entries below the diagonal are zero and the diagonal is positive.
All inputs are finite; a program needn't handle non-finite values.
Results may differ from a plain program's by a relative error of at most 0.0001.
Values sent between devices are 32-bit elements; how exact they have to be, the bound alone decides.
A program may use at most 64 MiB of HBM per device.

v0:
```python
import jax
import jax.numpy as jnp
from jax import lax
from jax.sharding import PartitionSpec as P

BLOCK = 64
ITERS = 3


def passed_along(value, axis, by):
    count = lax.axis_size(axis)
    pairs = [(i, i + by) for i in range(count) if 0 <= i + by < count]
    return lax.ppermute(value, axis, pairs)


def cayley(pair_gram):
    size_n = pair_gram.shape[0]
    diag_vals = jnp.diagonal(pair_gram)
    spread = diag_vals[:, None] - diag_vals[None, :]
    denom = 2.0 * (diag_vals[:, None] ** 2 + diag_vals[None, :] ** 2)
    skew_part = pair_gram * spread / denom
    unit_matrix = jnp.eye(size_n, dtype=pair_gram.dtype)
    minus_part = unit_matrix - skew_part
    system = unit_matrix - jnp.dot(skew_part, skew_part, precision=lax.Precision.HIGHEST)
    product = jnp.dot(minus_part, minus_part, precision=lax.Precision.HIGHEST)
    factor = jnp.linalg.cholesky(system)
    return jax.scipy.linalg.cho_solve((factor, True), product.T).T


def square_sums(rows_part):
    row_ids = jnp.arange(rows_part.shape[1], dtype=jnp.int32)[:, None]
    col_ids = jnp.arange(rows_part.shape[2], dtype=jnp.int32)[None, :]
    on_diag = (row_ids == col_ids)[None, :, :]
    squares = rows_part * rows_part
    return (jnp.sum(jnp.where(on_diag, 0.0, squares)), jnp.sum(jnp.where(on_diag, squares, 0.0)))


def on_device(r_factor, block_slots):
    rows_in, total_cols = r_factor.shape
    blocks = total_cols // BLOCK
    pair_width = 2 * BLOCK
    arranged = jnp.take(r_factor.reshape(rows_in, blocks, BLOCK), block_slots, axis=1)
    arranged = arranged.reshape(rows_in, blocks // 2, pair_width)
    received = lax.all_to_all(arranged, "pair", split_axis=1, concat_axis=0, tiled=True)
    column = jnp.transpose(received, (1, 0, 2))
    local_pairs = column.shape[0]
    rows_here = column.shape[1]
    totals = None
    for sweep in range(ITERS):
        partial_value = jnp.einsum("pri,prj->pij", column, column, precision=lax.Precision.HIGHEST)
        pair_gram = lax.psum(partial_value, "row")
        if sweep == 0:
            off_part, diag_part = square_sums(pair_gram)
            totals = lax.psum((off_part, diag_part), "pair")
        rotation = jax.vmap(cayley)(pair_gram)
        column = jnp.einsum("pri,pij->prj", column, rotation, precision=lax.Precision.HIGHEST)
    upper_half = column[:, :, :BLOCK]
    lower_half = column[:, :, BLOCK:]
    pair_index = lax.axis_index("pair")
    pair_count = lax.axis_size("pair")
    global_ids = pair_index * local_pairs + jnp.arange(local_pairs, dtype=jnp.int32)
    last_id = pair_count * local_pairs - 1
    first_mask = (global_ids == 0)[:, None, None]
    last_mask = (global_ids == last_id)[:, None, None]
    forward = jnp.where(first_mask, lower_half, upper_half)
    came_up = passed_along(forward[local_pairs - 1], "pair", 1)
    came_down = passed_along(lower_half[0], "pair", -1)
    before = jnp.concatenate([came_up[None], forward[: local_pairs - 1]], axis=0)
    after = jnp.concatenate([lower_half[1:], came_down[None]], axis=0)
    new_upper = jnp.where(first_mask, upper_half, before)
    new_lower = jnp.where(last_mask, upper_half, after)
    joined = jnp.concatenate([new_upper, new_lower], axis=2)
    rotated = jnp.transpose(joined, (1, 0, 2)).reshape(rows_here, local_pairs * pair_width)
    off_ratio = jnp.sqrt(totals[0] / totals[1])
    return (rotated, off_ratio)


def solution(mesh):
    in_specs = (P(("row", "pair"), None), P())
    out_specs = (P("row", "pair"), P())
    return jax.shard_map(
        on_device, mesh=mesh, in_specs=in_specs, out_specs=out_specs, check_vma=False
    )
```

profile of v0, /device:TPU:32, one launch (start us, length us, event | category | flops | bytes accessed | tf_op | source)
XLA Modules:
  0.0 870.0 jit_solution(1644041194459896223)
XLA Ops:
  7.2 0.7 compare_and_fusion
  7.9 0.7 compare_select_fusion
  8.9 4.3 reshape.87
  13.2 6.5 copy.172
  19.7 5.0 gather_fusion
  24.7 6.5 copy.173
  31.3 3.3 gather.17
  34.7 2.5 copy.174
  37.3 9.8 %all-to-all-start = ((f32[32,128,128]{2,0,1:T(8,128)}), f32[32,128,128]{2,0,1:T(8,128)S(1)}, u32[]{:S(2)}, u32[]{:S(2)}) async-start(f32[32,128,128]{2,0,1:T(8,128)} %copy.174), calls=%async_computation | async-start | bytes 4194304 | tf_op jit(solution)/shard_map/all_to_all | solution.py:44
  47.4 46.9 %all-to-all-done = f32[32,128,128]{2,0,1:T(8,128)S(1)} async-done(((f32[32,128,128]{2,0,1:T(8,128)}), f32[32,128,128]{2,0,1:T(8,128)S(1)}, u32[]{:S(2)}, u32[]{:S(2)}) %all-to-all-start) | async-done | bytes 2097184 | tf_op jit(solution)/shard_map/all_to_all | solution.py:44
  94.3 1.3 copy-done.3
  95.6 1.8 copy.175
  97.4 4.3 fusion.33
  101.8 119.5 %all-reduce.5.cloned.1.call-done = f32[4,128,128]{1,2,0:T(8,128)} async-done(((f32[4,128,128]{1,2,0:T(8,128)}), f32[4,128,128]{1,2,0:T(8,128)}) %all-reduce.5.cloned.1.call-update) | async-done | bytes 262160 | tf_op jit(solution)/shard_map/psum | solution.py:51
  221.3 8.5 copy.178
  229.7 1.8 gather_fusion.1
  231.6 0.7 convolution_subtract_fusion.2
  232.4 46.9 %custom-call.18 = f32[4,128,128]{2,1,0:T(8,128)S(1)} custom-call(f32[4,128,128]{2,1,0:T(8,128)S(1)} %fusion.14), custom_call_target="Cholesky" | custom-call | tf_op jit(solution)/shard_map/vmap(jit(cholesky))/cholesky | solution.py:26
  279.6 39.7 %custom-call.19 = f32[4,1,128,128]{2,3,1,0:T(8,128)S(1)} custom-call(f32[4,1,128,128]{3,2,1,0:T(8,128)S(1)} %select_bitcast_fusion.2), custom_call_target="InvertDiagBlocksLowerTriangular" | custom-call | tf_op jit(solution)/shard_map/vmap(jit(_cho_solve))/triangular_solve | solution.py:27
  321.0 1.9 fusion.34
  323.0 1.3 copy-done
  324.3 4.3 fusion.35
  328.6 116.2 %all-reduce.7.cloned.1.call-done = f32[4,128,128]{1,2,0:T(8,128)} async-done(((f32[4,128,128]{1,2,0:T(8,128)}), f32[4,128,128]{1,2,0:T(8,128)}) %all-reduce.7.cloned.1.call-update) | async-done | bytes 262160 | tf_op jit(solution)/shard_map/psum | solution.py:51
  444.8 8.5 copy.188
  453.3 1.8 gather_fusion.2
  455.2 0.7 convolution_subtract_fusion.1
  456.0 46.9 %custom-call.20 = f32[4,128,128]{2,1,0:T(8,128)S(1)} custom-call(f32[4,128,128]{2,1,0:T(8,128)S(1)} %fusion.9), custom_call_target="Cholesky" | custom-call | tf_op jit(solution)/shard_map/vmap(jit(cholesky))/cholesky | solution.py:26
  503.2 39.5 %custom-call.21 = f32[4,1,128,128]{2,3,1,0:T(8,128)S(1)} custom-call(f32[4,1,128,128]{3,2,1,0:T(8,128)S(1)} %select_bitcast_fusion.1), custom_call_target="InvertDiagBlocksLowerTriangular" | custom-call | tf_op jit(solution)/shard_map/vmap(jit(_cho_solve))/triangular_solve | solution.py:27
  544.4 3.5 fusion.36
  547.9 4.3 fusion.37
  552.2 116.0 %all-reduce.9.cloned.1.call-done = f32[4,128,128]{1,2,0:T(8,128)} async-done(((f32[4,128,128]{1,2,0:T(8,128)}), f32[4,128,128]{1,2,0:T(8,128)}) %all-reduce.9.cloned.1.call-update) | async-done | bytes 262160 | tf_op jit(solution)/shard_map/psum | solution.py:51
  668.3 8.5 copy.198
  676.7 1.8 gather_fusion.3
  678.6 0.7 convolution_subtract_fusion
  679.4 0.7 fusion.4
  680.1 47.9 %custom-call.22 = f32[4,128,128]{2,1,0:T(8,128)S(1)} custom-call(f32[4,128,128]{2,1,0:T(8,128)} %fusion.4), custom_call_target="Cholesky" | custom-call | tf_op jit(solution)/shard_map/vmap(jit(cholesky))/cholesky | solution.py:26
  728.3 39.3 %custom-call.23 = f32[4,1,128,128]{2,3,1,0:T(8,128)S(1)} custom-call(f32[4,1,128,128]{3,2,1,0:T(8,128)S(1)} %select_bitcast_fusion), custom_call_target="InvertDiagBlocksLowerTriangular" | custom-call | tf_op jit(solution)/shard_map/vmap(jit(_cho_solve))/triangular_solve | solution.py:27
  767.6 0.7 fusion.15
  769.3 2.0 fusion.38
  771.3 0.8 slice_bitcast_fusion
  772.1 4.6 collective-permute-start.1
  776.9 0.7 slice_bitcast_fusion.1
  777.6 1.9 collective-permute-start
  779.6 0.8 select_reduce_fusion.3
  780.4 75.6 %all-reduce = (f32[]{:T(128)}, f32[]{:T(128)}) all-reduce(f32[]{:T(128)} %get-tuple-element.15, f32[]{:T(128)} %get-tuple-element.14), channel_id=1, replica_groups=mesh['pair'=32,'row'=16] {'pair'}, use_global_device_ids=true, to_apply=%region_6.9 | all-reduce | flops 2 | bytes 16 | tf_op jit(solution)/shard_map/psum | solution.py:54
  857.2 1.2 slice.50
  858.5 1.4 maximum_select_fusion
  860.1 1.8 copy.206
  (64 shorter events, 7.2 us)
Async XLA Ops:
  37.3 57.0 %all-to-all-start = ((f32[32,128,128]{2,0,1:T(8,128)}), f32[32,128,128]{2,0,1:T(8,128)S(1)}, u32[]{:S(2)}, u32[]{:S(2)}) async-start(f32[32,128,128]{2,0,1:T(8,128)} %copy.174), calls=%async_computation | async-start | bytes 4194304 | tf_op jit(solution)/shard_map/all_to_all | solution.py:44
  47.1 174.2 %all-reduce.5.cloned.1.call-start = ((), (), s32[]{:S(2)}) async-start(), calls=%async_computation.1 | async-start | bytes 524288 | tf_op jit(solution)/shard_map/psum | solution.py:51
  94.3 1.3 copy-start.3
  101.7 343.1 %all-reduce.7.cloned.1.call-start = ((), (), s32[]{:S(2)}) async-start(), calls=%async_computation.2 | async-start | bytes 524288 | tf_op jit(solution)/shard_map/psum | solution.py:51
  221.3 10.3 %copy-start.4 = (f32[4,128,128]{1,2,0:T(8,128)S(1)}, f32[4,128,128]{1,2,0:T(8,128)}, u32[]{:S(2)}) copy-start(f32[4,128,128]{1,2,0:T(8,128)} %all-reduce.5.cloned.1.call-done) | copy-start | bytes 786436
  323.0 1.3 copy-start
  328.6 339.7 %all-reduce.9.cloned.1.call-start = ((), (), s32[]{:S(2)}) async-start(), calls=%async_computation.3 | async-start | bytes 524288 | tf_op jit(solution)/shard_map/psum | solution.py:51
  444.8 10.4 %copy-start.6 = (f32[4,128,128]{1,2,0:T(8,128)S(1)}, f32[4,128,128]{1,2,0:T(8,128)}, u32[]{:S(2)}) copy-start(f32[4,128,128]{1,2,0:T(8,128)} %all-reduce.7.cloned.1.call-done) | copy-start | bytes 786436
  668.3 10.3 %copy-start.5 = (f32[4,128,128]{1,2,0:T(8,128)S(1)}, f32[4,128,128]{1,2,0:T(8,128)}, u32[]{:S(2)}) copy-start(f32[4,128,128]{1,2,0:T(8,128)} %all-reduce.9.cloned.1.call-done) | copy-start | bytes 786436
  771.3 6.3 copy-start.1
  772.1 86.4 %collective-permute-start.1 = (f32[1024,64]{0,1:T(8,128)}, f32[1024,64]{0,1:T(8,128)}, u32[]{:S(2)}, u32[]{:S(2)}) collective-permute-start(f32[1024,64]{0,1:T(8,128)} %slice_bitcast_fusion), channel_id=1, source_target_pairs={{16,0},{32,16},{48,32},{64,48},{80,64},{96,80},{112,96},{128,112},... | collective-permute-start | bytes 786440 | tf_op jit(solution)/shard_map/ppermute | solution.py:13
  777.6 80.9 %collective-permute-start = (f32[1024,64]{0,1:T(8,128)}, f32[1024,64]{0,1:T(8,128)}, u32[]{:S(2)}, u32[]{:S(2)}) collective-permute-start(f32[1024,64]{0,1:T(8,128)} %slice_bitcast_fusion.1), channel_id=1, source_target_pairs={{0,16},{16,32},{32,48},{48,64},{64,80},{80,96},{96,112},{112,128},... | collective-permute-start | bytes 786440 | tf_op jit(solution)/shard_map/ppermute | solution.py:13
  779.5 79.0 %copy-start.2 = (f32[4,1024,128]{1,2,0:T(8,128)S(1)}, f32[4,1024,128]{1,2,0:T(8,128)}, u32[]{:S(2)}) copy-start(f32[4,1024,128]{1,2,0:T(8,128)} %copy-done.1) | copy-start | bytes 6291460
Sparse Core Ops, SparseCore 0:
  101.8 119.4 all-reduce.4
  328.7 116.0 all-reduce.6
  552.3 115.8 all-reduce.8
where the time goes:
time: 877 us; the launch traced here: 870 us
  waiting for transfers between devices  399 us (45%)
  other arithmetic  266 us (30%)
  blocking collectives  75.6 us (9%)
  local copies, waits for them, and re-layouts  68.9 us (8%)
  matrix products  27.1 us (3%)
  between operations  17 us (2%)
  starting transfers between devices  16.6 us (2%)
    psum x3, waiting for transfers between devices, on_device(): pair_gram = lax.psum(partial_value, 'row')  352 us
    another operation x10, other arithmetic, cayley(): factor = jnp.linalg.cholesky(system)  142 us
    another operation x7, other arithmetic, cayley(): return jax.scipy.linalg.cho_solve((factor, True), product.T).T  119 us
    psum x1, blocking collectives, on_device(): totals = lax.psum((off_part, diag_part), 'pair')  75.6 us
    all_to_all x1, waiting for transfers between devices, on_device(): lax.all_to_all(arranged, 'pair', split_axis=1, concat_axis=0, tiled=True)  46.9 us
    psum x3, local copies, waits for them, and re-layouts, on_device(): pair_gram = lax.psum(partial_value, 'row')  25.4 us
  transfers between devices with their start and end apart: 6, of which 4 were waited for; matrix products, arithmetic and copies ran while one was open for 0% of the time, Pallas kernels for 0%

commit v1 on v0

--- a/solution.py
+++ b/solution.py
@@ -5,6 +5,14 @@
 
 BLOCK = 64
 ITERS = 3
+
+
+def add_in_pairs(array, axis):
+    size, total = (lax.axis_size(axis), array)
+    for far in [1 << k for k in range(size.bit_length() - 1)]:
+        swap = [(i, i ^ far) for i in range(size)]
+        total = total + lax.ppermute(total, axis, swap)
+    return total
 
 
 def passed_along(value, axis, by):
@@ -48,7 +56,7 @@
     totals = None
     for sweep in range(ITERS):
         partial_value = jnp.einsum("pri,prj->pij", column, column, precision=lax.Precision.HIGHEST)
-        pair_gram = lax.psum(partial_value, "row")
+        pair_gram = add_in_pairs(partial_value, "row")
         if sweep == 0:
             off_part, diag_part = square_sums(pair_gram)
             totals = lax.psum((off_part, diag_part), "pair")

time: 877 us -> 652 us (0.74)
  waiting for transfers between devices: 399 us -> 101 us
  blocking collectives: 75.6 us -> 131 us
  starting transfers between devices: 16.6 us -> 57.5 us
  between operations: 17 us -> 4.18 us
    psum x3 -> x0, waiting for transfers between devices: 352 us -> none  [on_device(): pair_gram = lax.psum(partial_value, 'row')]
    ppermute x0 -> x12, waiting for transfers between devices: none -> 101 us  [add_in_pairs(): total = total + lax.ppermute(total, axis, swap)]
    all_to_all x0 -> x1, blocking collectives: none -> 57.5 us  [on_device(): lax.all_to_all(arranged, 'pair', split_axis=1, concat_axis=0, tiled=True)]
    ppermute x0 -> x12, starting transfers between devices: none -> 48.2 us  [add_in_pairs(): total = total + lax.ppermute(total, axis, swap)]
    all_to_all x1 -> x0, waiting for transfers between devices: 46.9 us -> none  [on_device(): lax.all_to_all(arranged, 'pair', split_axis=1, concat_axis=0, tiled=True)]
    psum x3 -> x0, local copies, waits for them, and re-layouts: 25.4 us -> none  [on_device(): pair_gram = lax.psum(partial_value, 'row')]
    add x0 -> x3, local copies, waits for them, and re-layouts: none -> 23.1 us  [add_in_pairs(): total = total + lax.ppermute(total, axis, swap)]
    all_to_all x1 -> x0, starting transfers between devices: 9.83 us -> none  [on_device(): lax.all_to_all(arranged, 'pair', split_axis=1, concat_axis=0, tiled=True)]
  transfers between devices with their start and end apart: 6 -> 14, of which waited for: 4 -> 12; matrix products, arithmetic and copies ran while one was open for 0% -> 0% of each run, Pallas kernels for 0% -> 0%
where the time goes in v1:
time: 652 us; the launch traced here: 644 us
  other arithmetic  265 us (41%)
  blocking collectives  131 us (20%)
  waiting for transfers between devices  101 us (15%)
  local copies, waits for them, and re-layouts  60.9 us (9%)
  starting transfers between devices  57.5 us (9%)
  matrix products  25.1 us (4%)
    another operation x10, other arithmetic, cayley(): factor = jnp.linalg.cholesky(system)  141 us
    another operation x7, other arithmetic, cayley(): return jax.scipy.linalg.cho_solve((factor, True), product.T).T  119 us
    ppermute x12, waiting for transfers between devices, add_in_pairs(): total = total + lax.ppermute(total, axis, swap)  101 us
    psum x1, blocking collectives, on_device(): totals = lax.psum((off_part, diag_part), 'pair')  73.5 us
    all_to_all x1, blocking collectives, on_device(): lax.all_to_all(arranged, 'pair', split_axis=1, concat_axis=0, tiled=True)  57.5 us
    ppermute x12, starting transfers between devices, add_in_pairs(): total = total + lax.ppermute(total, axis, swap)  48.2 us
    add x3, local copies, waits for them, and re-layouts, add_in_pairs(): total = total + lax.ppermute(total, axis, swap)  23.1 us
    gather x3, local copies, waits for them, and re-layouts, on_device(): jnp.take(r_factor.reshape(rows_in, blocks, BLOCK), block_slots, axis=1)  14.8 us
  transfers between devices with their start and end apart: 14, of which 12 were waited for; matrix products, arithmetic and copies ran while one was open for 0% of the time, Pallas kernels for 0%

profile of v1, /device:TPU:32, one launch (start us, length us, event | category | flops | bytes accessed | tf_op | source)
XLA Modules:
  0.0 644.2 jit_solution(1936622645766868482)
XLA Ops:
  2.0 4.3 reshape.87
  6.3 6.5 %copy.184 = f32[32,256,64]{2,0,1:T(8,128)} copy(f32[32,256,64]{2,1,0:T(8,128)} %reshape.87) | data formatting | bytes 4194304 | tf_op jit(solution)/shard_map/reshape | solution.py:50
  12.8 5.0 gather_fusion
  17.8 6.5 %copy.185 = f32[32,256,64]{2,1,0:T(8,128)} copy(f32[32,256,64]{2,0,1:T(8,128)} %bitcast.78) | data formatting | bytes 4194304 | tf_op jit(solution)/shard_map/jit(_take)/gather | solution.py:50
  24.3 3.3 gather.17
  29.4 57.5 %all_to_all.18 = f32[32,128,128]{2,0,1:T(8,128)S(1)} all-to-all(f32[32,128,128]{2,0,1:T(8,128)S(1)} %copy.186), channel_id=1, replica_groups=mesh['pair'=32,'row'=16] {'pair'}, dimensions={1} | all-to-all | bytes 4194304 | tf_op jit(solution)/shard_map/all_to_all | solution.py:52
  87.1 3.6 fusion.33
  90.7 1.9 collective-permute-start
  94.1 4.3 collective-permute-start.1
  98.4 6.6 %collective-permute-done.1 = f32[4,128,128]{1,2,0:T(8,128)S(1)} collective-permute-done((f32[4,128,128]{1,2,0:T(8,128)S(1)}, f32[4,128,128]{1,2,0:T(8,128)S(1)}, u32[]{:S(2)}, u32[]{:S(2)}) %collective-permute-start.1) | collective-permute-done | bytes 262176 | tf_op jit(solution)/shard_map/ppermute | solution.py:14
  105.1 6.1 collective-permute-start.2
  111.2 11.6 %collective-permute-done.2 = f32[4,128,128]{1,2,0:T(8,128)S(1)} collective-permute-done((f32[4,128,128]{1,2,0:T(8,128)S(1)}, f32[4,128,128]{1,2,0:T(8,128)S(1)}, u32[]{:S(2)}, u32[]{:S(2)}) %collective-permute-start.2) | collective-permute-done | bytes 262176 | tf_op jit(solution)/shard_map/ppermute | solution.py:14
  122.8 8.5 %collective-permute-start.3 = (f32[4,128,128]{1,2,0:T(8,128)S(1)}, f32[4,128,128]{1,2,0:T(8,128)S(1)}, u32[]{:S(2)}, u32[]{:S(2)}) collective-permute-start(f32[4,128,128]{1,2,0:T(8,128)S(1)} %add.125), channel_id=1, source_target_pairs={{0,8},{1,9},{2,10},{3,11},{4,12},{5,13},{6,14},{7,15},{8,0},{9,1},... | collective-permute-start | bytes 786440 | tf_op jit(solution)/shard_map/ppermute | solution.py:14
  131.3 11.2 %collective-permute-done.3 = f32[4,128,128]{1,2,0:T(8,128)S(1)} collective-permute-done((f32[4,128,128]{1,2,0:T(8,128)S(1)}, f32[4,128,128]{1,2,0:T(8,128)S(1)}, u32[]{:S(2)}, u32[]{:S(2)}) %collective-permute-start.3) | collective-permute-done | bytes 262176 | tf_op jit(solution)/shard_map/ppermute | solution.py:14
  143.2 7.5 %copy.191 = f32[4,128,128]{0,2,1:T(8,128)} copy(f32[4,128,128]{1,2,0:T(8,128)S(1)} %get-tuple-element.18) | data formatting | bytes 524288 | tf_op jit(solution)/shard_map/add | solution.py:14
  150.8 1.8 gather_fusion.1
  154.1 46.9 %custom-call.18 = f32[4,128,128]{2,1,0:T(8,128)S(1)} custom-call(f32[4,128,128]{2,1,0:T(8,128)S(1)} %fusion.14), custom_call_target="Cholesky" | custom-call | tf_op jit(solution)/shard_map/vmap(jit(cholesky))/cholesky | solution.py:34
  201.3 39.7 %custom-call.19 = f32[4,1,128,128]{2,3,1,0:T(8,128)S(1)} custom-call(f32[4,1,128,128]{3,2,1,0:T(8,128)S(1)} %select_bitcast_fusion.2), custom_call_target="InvertDiagBlocksLowerTriangular" | custom-call | tf_op jit(solution)/shard_map/vmap(jit(_cho_solve))/triangular_solve | solution.py:35
  242.0 1.9 fusion.34
  244.0 3.6 fusion.35
  247.5 1.9 collective-permute-start.4
  251.0 1.9 collective-permute-start.5
  252.9 8.3 %collective-permute-done.5 = f32[4,128,128]{1,2,0:T(8,128)S(1)} collective-permute-done((f32[4,128,128]{1,2,0:T(8,128)S(1)}, f32[4,128,128]{1,2,0:T(8,128)S(1)}, u32[]{:S(2)}, u32[]{:S(2)}) %collective-permute-start.5) | collective-permute-done | bytes 262176 | tf_op jit(solution)/shard_map/ppermute | solution.py:14
  261.3 4.9 collective-permute-start.6
  266.2 11.6 %collective-permute-done.6 = f32[4,128,128]{1,2,0:T(8,128)S(1)} collective-permute-done((f32[4,128,128]{1,2,0:T(8,128)S(1)}, f32[4,128,128]{1,2,0:T(8,128)S(1)}, u32[]{:S(2)}, u32[]{:S(2)}) %collective-permute-start.6) | collective-permute-done | bytes 262176 | tf_op jit(solution)/shard_map/ppermute | solution.py:14
  277.8 4.8 collective-permute-start.7
  282.6 13.5 %collective-permute-done.7 = f32[4,128,128]{1,2,0:T(8,128)S(1)} collective-permute-done((f32[4,128,128]{1,2,0:T(8,128)S(1)}, f32[4,128,128]{1,2,0:T(8,128)S(1)}, u32[]{:S(2)}, u32[]{:S(2)}) %collective-permute-start.7) | collective-permute-done | bytes 262176 | tf_op jit(solution)/shard_map/ppermute | solution.py:14
  296.1 7.7 %copy.202 = f32[4,128,128]{0,2,1:T(8,128)} copy(f32[4,128,128]{1,2,0:T(8,128)S(1)} %add.133) | data formatting | bytes 524288 | tf_op jit(solution)/shard_map/add | solution.py:14
  303.9 1.8 gather_fusion.2
  307.2 46.9 %custom-call.20 = f32[4,128,128]{2,1,0:T(8,128)S(1)} custom-call(f32[4,128,128]{2,1,0:T(8,128)S(1)} %fusion.9), custom_call_target="Cholesky" | custom-call | tf_op jit(solution)/shard_map/vmap(jit(cholesky))/cholesky | solution.py:34
  354.4 39.5 %custom-call.21 = f32[4,1,128,128]{2,3,1,0:T(8,128)S(1)} custom-call(f32[4,1,128,128]{3,2,1,0:T(8,128)S(1)} %select_bitcast_fusion.1), custom_call_target="InvertDiagBlocksLowerTriangular" | custom-call | tf_op jit(solution)/shard_map/vmap(jit(_cho_solve))/triangular_solve | solution.py:35
  394.9 3.5 fusion.36
  398.5 3.6 fusion.37
  402.0 1.9 collective-permute-start.8
  405.5 1.9 collective-permute-start.9
  407.4 8.3 %collective-permute-done.9 = f32[4,128,128]{1,2,0:T(8,128)S(1)} collective-permute-done((f32[4,128,128]{1,2,0:T(8,128)S(1)}, f32[4,128,128]{1,2,0:T(8,128)S(1)}, u32[]{:S(2)}, u32[]{:S(2)}) %collective-permute-start.9) | collective-permute-done | bytes 262176 | tf_op jit(solution)/shard_map/ppermute | solution.py:14
  415.8 5.1 collective-permute-start.10
  420.9 11.6 %collective-permute-done.10 = f32[4,128,128]{1,2,0:T(8,128)S(1)} collective-permute-done((f32[4,128,128]{1,2,0:T(8,128)S(1)}, f32[4,128,128]{1,2,0:T(8,128)S(1)}, u32[]{:S(2)}, u32[]{:S(2)}) %collective-permute-start.10) | collective-permute-done | bytes 262176 | tf_op jit(solution)/shard_map/ppermute | solution.py:14
  432.6 5.0 collective-permute-start.11
  437.6 13.4 %collective-permute-done.11 = f32[4,128,128]{1,2,0:T(8,128)S(1)} collective-permute-done((f32[4,128,128]{1,2,0:T(8,128)S(1)}, f32[4,128,128]{1,2,0:T(8,128)S(1)}, u32[]{:S(2)}, u32[]{:S(2)}) %collective-permute-start.11) | collective-permute-done | bytes 262176 | tf_op jit(solution)/shard_map/ppermute | solution.py:14
  451.1 7.8 %copy.213 = f32[4,128,128]{0,2,1:T(8,128)} copy(f32[4,128,128]{1,2,0:T(8,128)S(1)} %add.140) | data formatting | bytes 524288 | tf_op jit(solution)/shard_map/add | solution.py:14
  462.2 46.9 %custom-call.22 = f32[4,128,128]{2,1,0:T(8,128)S(1)} custom-call(f32[4,128,128]{2,1,0:T(8,128)S(1)} %fusion.4), custom_call_target="Cholesky" | custom-call | tf_op jit(solution)/shard_map/vmap(jit(cholesky))/cholesky | solution.py:34
  509.4 39.6 %custom-call.23 = f32[4,1,128,128]{2,3,1,0:T(8,128)S(1)} custom-call(f32[4,1,128,128]{3,2,1,0:T(8,128)S(1)} %select_bitcast_fusion), custom_call_target="InvertDiagBlocksLowerTriangular" | custom-call | tf_op jit(solution)/shard_map/vmap(jit(_cho_solve))/triangular_solve | solution.py:35
  550.0 2.0 fusion.38
  553.8 2.3 collective-permute-start.12
  556.1 6.9 %collective-permute-start.13 = (f32[1024,64]{0,1:T(8,128)}, f32[1024,64]{0,1:T(8,128)}, u32[]{:S(2)}, u32[]{:S(2)}) collective-permute-start(f32[1024,64]{0,1:T(8,128)} %slice_bitcast_fusion), channel_id=1, source_target_pairs={{16,0},{32,16},{48,32},{64,48},{80,64},{96,80},{112,96},{128,112},... | collective-permute-start | bytes 786440 | tf_op jit(solution)/shard_map/ppermute | solution.py:21
  563.1 73.5 %all-reduce = (f32[]{:T(128)}, f32[]{:T(128)}) all-reduce(f32[]{:T(128)} %get-tuple-element.15, f32[]{:T(128)} %get-tuple-element.14), channel_id=1, replica_groups=mesh['pair'=32,'row'=16] {'pair'}, use_global_device_ids=true, to_apply=%region_3.6 | all-reduce | flops 2 | bytes 16 | tf_op jit(solution)/shard_map/psum | solution.py:62
  640.8 1.8 copy.221
  (81 shorter events, 23.6 us)
Async XLA Ops:
  90.7 3.4 collective-permute-start
  94.1 10.9 %collective-permute-start.1 = (f32[4,128,128]{1,2,0:T(8,128)S(1)}, f32[4,128,128]{1,2,0:T(8,128)S(1)}, u32[]{:S(2)}, u32[]{:S(2)}) collective-permute-start(f32[4,128,128]{1,2,0:T(8,128)S(1)} %add.123), channel_id=1, source_target_pairs={{0,2},{1,3},{2,0},{3,1},{4,6},{5,7},{6,4},{7,5},{8,10},{9,11},{10,... | collective-permute-start | bytes 786440 | tf_op jit(solution)/shard_map/ppermute | solution.py:14
  105.1 17.7 %collective-permute-start.2 = (f32[4,128,128]{1,2,0:T(8,128)S(1)}, f32[4,128,128]{1,2,0:T(8,128)S(1)}, u32[]{:S(2)}, u32[]{:S(2)}) collective-permute-start(f32[4,128,128]{1,2,0:T(8,128)S(1)} %add.124), channel_id=1, source_target_pairs={{0,4},{1,5},{2,6},{3,7},{4,0},{5,1},{6,2},{7,3},{8,12},{9,13},{10,... | collective-permute-start | bytes 786440 | tf_op jit(solution)/shard_map/ppermute | solution.py:14
  122.8 19.7 %collective-permute-start.3 = (f32[4,128,128]{1,2,0:T(8,128)S(1)}, f32[4,128,128]{1,2,0:T(8,128)S(1)}, u32[]{:S(2)}, u32[]{:S(2)}) collective-permute-start(f32[4,128,128]{1,2,0:T(8,128)S(1)} %add.125), channel_id=1, source_target_pairs={{0,8},{1,9},{2,10},{3,11},{4,12},{5,13},{6,14},{7,15},{8,0},{9,1},... | collective-permute-start | bytes 786440 | tf_op jit(solution)/shard_map/ppermute | solution.py:14
  244.0 3.6 copy-start
  247.5 3.4 collective-permute-start.4
  251.0 10.2 %collective-permute-start.5 = (f32[4,128,128]{1,2,0:T(8,128)S(1)}, f32[4,128,128]{1,2,0:T(8,128)S(1)}, u32[]{:S(2)}, u32[]{:S(2)}) collective-permute-start(f32[4,128,128]{1,2,0:T(8,128)S(1)} %add.130), channel_id=1, source_target_pairs={{0,2},{1,3},{2,0},{3,1},{4,6},{5,7},{6,4},{7,5},{8,10},{9,11},{10,... | collective-permute-start | bytes 786440 | tf_op jit(solution)/shard_map/ppermute | solution.py:14
  261.3 16.5 %collective-permute-start.6 = (f32[4,128,128]{1,2,0:T(8,128)S(1)}, f32[4,128,128]{1,2,0:T(8,128)S(1)}, u32[]{:S(2)}, u32[]{:S(2)}) collective-permute-start(f32[4,128,128]{1,2,0:T(8,128)S(1)} %add.131), channel_id=1, source_target_pairs={{0,4},{1,5},{2,6},{3,7},{4,0},{5,1},{6,2},{7,3},{8,12},{9,13},{10,... | collective-permute-start | bytes 786440 | tf_op jit(solution)/shard_map/ppermute | solution.py:14
  277.8 18.2 %collective-permute-start.7 = (f32[4,128,128]{1,2,0:T(8,128)S(1)}, f32[4,128,128]{1,2,0:T(8,128)S(1)}, u32[]{:S(2)}, u32[]{:S(2)}) collective-permute-start(f32[4,128,128]{1,2,0:T(8,128)S(1)} %add.132), channel_id=1, source_target_pairs={{0,8},{1,9},{2,10},{3,11},{4,12},{5,13},{6,14},{7,15},{8,0},{9,1},... | collective-permute-start | bytes 786440 | tf_op jit(solution)/shard_map/ppermute | solution.py:14
  402.0 3.4 collective-permute-start.8
  405.5 10.2 %collective-permute-start.9 = (f32[4,128,128]{1,2,0:T(8,128)S(1)}, f32[4,128,128]{1,2,0:T(8,128)S(1)}, u32[]{:S(2)}, u32[]{:S(2)}) collective-permute-start(f32[4,128,128]{1,2,0:T(8,128)S(1)} %add.137), channel_id=1, source_target_pairs={{0,2},{1,3},{2,0},{3,1},{4,6},{5,7},{6,4},{7,5},{8,10},{9,11},{10,... | collective-permute-start | bytes 786440 | tf_op jit(solution)/shard_map/ppermute | solution.py:14
  415.8 16.8 %collective-permute-start.10 = (f32[4,128,128]{1,2,0:T(8,128)S(1)}, f32[4,128,128]{1,2,0:T(8,128)S(1)}, u32[]{:S(2)}, u32[]{:S(2)}) collective-permute-start(f32[4,128,128]{1,2,0:T(8,128)S(1)} %add.138), channel_id=1, source_target_pairs={{0,4},{1,5},{2,6},{3,7},{4,0},{5,1},{6,2},{7,3},{8,12},{9,13},{10,... | collective-permute-start | bytes 786440 | tf_op jit(solution)/shard_map/ppermute | solution.py:14
  432.6 18.4 %collective-permute-start.11 = (f32[4,128,128]{1,2,0:T(8,128)S(1)}, f32[4,128,128]{1,2,0:T(8,128)S(1)}, u32[]{:S(2)}, u32[]{:S(2)}) collective-permute-start(f32[4,128,128]{1,2,0:T(8,128)S(1)} %add.139), channel_id=1, source_target_pairs={{0,8},{1,9},{2,10},{3,11},{4,12},{5,13},{6,14},{7,15},{8,0},{9,1},... | collective-permute-start | bytes 786440 | tf_op jit(solution)/shard_map/ppermute | solution.py:14
  552.0 1.7 copy-start.1
  553.8 85.5 %collective-permute-start.12 = (f32[1024,64]{0,1:T(8,128)}, f32[1024,64]{0,1:T(8,128)S(1)}, u32[]{:S(2)}, u32[]{:S(2)}) collective-permute-start(f32[1024,64]{0,1:T(8,128)} %slice_bitcast_fusion.1), channel_id=1, source_target_pairs={{0,16},{16,32},{32,48},{48,64},{64,80},{80,96},{96,112},{112,128},... | collective-permute-start | bytes 786440 | tf_op jit(solution)/shard_map/ppermute | solution.py:21
  556.1 83.2 %copy-start.2 = (f32[4,1024,128]{1,2,0:T(8,128)S(1)}, f32[4,1024,128]{1,2,0:T(8,128)}, u32[]{:S(2)}) copy-start(f32[4,1024,128]{1,2,0:T(8,128)} %copy-done.1) | copy-start | bytes 6291460
  556.1 83.1 %collective-permute-start.13 = (f32[1024,64]{0,1:T(8,128)}, f32[1024,64]{0,1:T(8,128)}, u32[]{:S(2)}, u32[]{:S(2)}) collective-permute-start(f32[1024,64]{0,1:T(8,128)} %slice_bitcast_fusion), channel_id=1, source_target_pairs={{16,0},{32,16},{48,32},{64,48},{80,64},{96,80},{112,96},{128,112},... | collective-permute-start | bytes 786440 | tf_op jit(solution)/shard_map/ppermute | solution.py:21
